TPU v7x, 768 devices: a whole 4x8x12 slice. The times are simulated.
768 devices in a mesh: tile: 32 (over x_hi, y, core), trc: 24 (over x_lo, z).
Axes of the slice: x: 4 (x_hi: 2, x_lo: 2; x = x_hi * 2 + x_lo), y: 8, z: 12, core: 2. Of those that a mesh axis runs over, the one named last changes fastest.
Arguments:
- tracers: float32 [96, 8, 256, 128], P('trc', None, 'tile'), may hold values from -6 to 6
- flux_pool: float32 [24, 2, 3, 8, 256, 128], P('trc', None, None, None, 'tile'), may hold values from -0.45 to 0.45
- mass_pool: float32 [24, 2, 8, 256, 128], P('trc', None, None, 'tile'), may hold values from 1 to 2
- owner: int32 [2, 32], P(None, 'tile'), may hold values from 0 to 23
- conv_cols: int32 [32, 256], P('tile'), may hold values from 0 to 1023, as said below
- conv_steps: int32 [32, 256], P('tile'), may hold values from 1 to 3
- conv_rate: float32 [32, 7, 256], P('tile'), may hold values from 0.05 to 0.5
Outputs:
- advected: float32 [96, 8, 256, 128], P('trc', None, 'tile')
Inputs may be any that keep to these rules, and one draw needn't show every extreme that they name: `conv_cols`: the 256 columns listed for one tile are all different.
All inputs are finite; a program needn't handle non-finite values.
Results may differ from a plain program's by a relative error of at most 0.0003.
Values sent between devices are 32-bit elements; how exact they have to be, the bound alone decides.
No kernel may reach another device: no remote copies, remote signals or barrier semaphores. Data moves between devices by JAX's collectives and lax.ppermute only.
A program may use at most 32 MiB of HBM per device.

v0:
```python
import functools

import jax
import jax.numpy as jnp
from jax import lax
from jax.experimental import pallas as pl
from jax.experimental.pallas import tpu as pltpu
from jax.sharding import Mesh, PartitionSpec as P

TILE = ("x_hi", "y", "core")
TRC = ("x_lo", "za", "zb")
NEAR = ("x_lo", "zb")
VM = pl.BlockSpec(memory_space=pltpu.VMEM)
F32 = jnp.float32


def shaped(*shape, dtype=F32):
    return pltpu.VMEM(shape, dtype)


def call(kernel, outs, *args, scratch=(), flops=20000, near=True):
    size = sum(4 * a.size for a in args)
    return pl.pallas_call(
        kernel,
        out_shape=outs,
        in_specs=[VM] * len(args),
        out_specs=jax.tree.map(lambda _: VM, outs),
        scratch_shapes=list(scratch),
        cost_estimate=pl.CostEstimate(flops=flops, bytes_accessed=size, transcendentals=0),
    )(*[pltpu.with_memory_space_constraint(a, pltpu.VMEM) if near else a for a in args])


def column(ref, first, x):
    return ref[pl.ds(first + x, 8, stride=8), :]


def pack_kernel(flux_ref, mass_ref, owner_ref, cols_ref, steps_ref, rate_ref, out_ref, owner_out, dense_ref):
    for s in range(2):
        for x in range(8):
            for f in range(3):
                out_ref[32 * s + 8 * f + x] = column(flux_ref, (s * 3 + f) * 64, x)
            out_ref[32 * s + 24 + x] = column(mass_ref, s * 64, x)
    first = lax.axis_index("x_lo") == 0
    owner = jnp.broadcast_to(jnp.where(first, owner_ref[0:1, 0:1], owner_ref[0:1, 1:2]), (8, 128))
    owner_out[0] = 4 * (owner // 12) + owner % 4
    owner_out[1] = (owner % 12) // 4
    cols = cols_ref[...]
    at_x, at_y = cols // 128, cols % 128
    values = jnp.concatenate([steps_ref[...].astype(F32), rate_ref[:, 0, :]], axis=0)
    weights = jnp.concatenate([jnp.where(at_x == x, values, 0.0) for x in range(8)], axis=0)
    hot = jnp.where(lax.broadcasted_iota(jnp.int32, (128, cols.shape[1]), 0) == at_y, 1.0, 0.0)
    dense = lax.dot_general(
        weights, hot, (((1,), (1,)), ((), ())),
        precision=lax.Precision.HIGHEST, preferred_element_type=F32,
    )
    dense_ref[...] = dense.reshape(dense_ref.shape)


def pick_kernel(owner_ref, got_ref, out_ref, *, which):
    owner = owner_ref[which]
    copies = out_ref.shape[0] // 8
    for n in range(8):
        value = got_ref[n]
        for m in range(1, got_ref.shape[0] // 8):
            value = jnp.where(owner == m, got_ref[8 * m + n], value)
        for m in range(copies):
            out_ref[8 * m + n] = value


def rows(n):
    return pl.ds(8 * n if isinstance(n, int) else pl.multiple_of(8 * n, 8), 8), slice(None)


FX, FY, FZ, MASS = range(4)
HALO = [(FX, 0, 4), (MASS, 0, 4), (FY, 0, 3), (FZ, 0, 3), (FX, 1, 1), (MASS, 1, 1)]
BODY = 27
SENT = BODY + sum(k for _, _, k in HALO)


def fill_body(out, last, tracers_ref, conv_ref):
    for i in range(4):
        for n in range(6):
            out[6 * i + n] = column(tracers_ref, 64 * i, 2 * last + n)
    for n in range(3):
        out[24 + n] = conv_ref[5 * last + n]


def fill_met(out, at, last, met_ref):
    for field, step, k in HALO:
        for n in range(k):
            out[at + n] = met_ref[32 * step + 8 * field + (8 - k) * last + n]
        at += k


def send_body_kernel(tracers_ref, conv_ref, far_ref, mate_ref):
    core = lax.axis_index("core")
    fill_body(far_ref, core, tracers_ref, conv_ref)
    fill_body(mate_ref, 1 - core, tracers_ref, conv_ref)


def send_met_kernel(met_ref, body_ref, far_ref, mate_ref):
    core = lax.axis_index("core")
    fill_met(far_ref, 0, core, met_ref)
    for n in range(BODY):
        mate_ref[n] = body_ref[n]
    fill_met(mate_ref, BODY, 1 - core, met_ref)


def clipped(value, bound):
    return jnp.maximum(jnp.minimum(value, jnp.maximum(bound, 0.0)), jnp.minimum(bound, 0.0))


def edge_offset(before, here, after):
    return clipped(0.5 * here + (1.0 / 12.0) * (before - after), here)


def limited(u, v):
    return clipped(u, v + v), clipped(v, u + u)


def face_factors(flux, near, far):
    size = jnp.abs(flux)
    share = size * jnp.where(flux > 0.0, near, far)
    rest = size * (1.0 - share)
    return rest * (1.0 - share), rest * share


def sweep_y(q, flux, k1, k2, per_mass, open_face):
    def ahead(x):
        return pltpu.roll(x, 127, 1)

    def behind(x):
        return pltpu.roll(x, 1, 1)

    q_next = ahead(q)
    diff = jnp.where(open_face, q_next - q, 0.0)
    u = edge_offset(behind(diff), diff, ahead(diff))
    v = behind(diff - u)
    u, v = limited(u, v)
    forward = flux > 0.0
    transport = (
        flux * jnp.where(forward, q, q_next)
        + k1 * jnp.where(forward, u, ahead(v))
        + k2 * jnp.where(forward, v, ahead(u))
    )
    return q - (transport - behind(transport)) * per_mass


def sweep_z(q, faces, per_mass):
    diff = [q[k + 1] - q[k] for k in range(7)]
    zero = jnp.zeros_like(q[0])
    u, v = [zero] * 8, [zero] * 8
    edge, rest = {}, {}
    for k in range(7):
        slope = diff[k - 1] - diff[k + 1] if 0 < k < 6 else (-diff[1] if k == 0 else diff[5])
        edge[k] = clipped(0.5 * diff[k] + (1.0 / 12.0) * slope, diff[k])
        rest[k + 1] = diff[k] - edge[k]
        if k > 0:
            u[k], v[k] = limited(edge[k], rest[k])
    out, before = [], None
    for k in range(8):
        if k < 7:
            flux, k1, k2 = faces(k)
            forward = flux > 0.0
            sent = (
                flux * jnp.where(forward, q[k], q[k + 1])
                + k1 * jnp.where(forward, u[k], v[k + 1])
                + k2 * jnp.where(forward, v[k], u[k + 1])
            )
            change = sent if before is None else sent - before
            before = sent
        else:
            change = -before
        out.append(q[k] - change * per_mass(k))
    return out


def stage(wide, cells, tables, met_ref, tracers_ref, conv_ref, halos):
    for bulk, got, right in halos:
        if cells is not None:
            for i in range(4):
                for n in range(6):
                    cells[rows(20 * i + 14 * right + n)] = bulk(6 * i + n)
            for n in range(3):
                tables[rows(11 * right + n)] = bulk(24 + n)
        at = 0
        for field, step, k in HALO:
            if (field, step) in wide:
                for n in range(k):
                    wide[field, step][rows((8 + k) * right + n)] = got(at + n)
            at += k
    for x in range(8):
        if cells is not None:
            for i in range(4):
                cells[rows(20 * i + 6 + x)] = column(tracers_ref, 64 * i, x)
            tables[rows(3 + x)] = conv_ref[x]
        for field, step, k in HALO:
            if (field, step) in wide:
                wide[field, step][rows(k + x)] = met_ref[rows(32 * step + 8 * field + x)]


def level(ref, first, k):
    return ref[pl.ds(8 * first + k, 8, stride=8), :]


def advance(count, shift, cell, flux_x, mass, flux_y, flux_z, tables, window, emit, swept, factors, per_mass, lines):
    for n in range(count + 2):
        per_mass[rows(n + 2)] = 1.0 / mass(n)
    for n in range(count + 1):
        flux = flux_x(n)
        k1, k2 = face_factors(flux, per_mass[rows(n + 2)], per_mass[rows(n + 3)])
        factors[0, n], factors[1, n], factors[2, n] = flux, k1, k2

    for i in range(4):
        q, diff, u, v, sent = {}, {}, {}, {}, {}
        for e in range(-3, count + 3):
            q[e] = cell(i, e + 3)
            if e - 1 in q:
                diff[e - 1] = q[e] - q[e - 1]
            if e - 3 in diff:
                u[e - 2] = edge_offset(diff[e - 3], diff[e - 2], diff[e - 1])
                v[e - 1] = diff[e - 2] - u[e - 2]
            j = e - 2
            if j in v:
                u[j], v[j] = limited(u[j], v[j])
            j = e - 3
            if -1 <= j < count:
                flux = factors[0, j + 1]
                forward = flux > 0.0
                sent[j] = (
                    flux * jnp.where(forward, q[j], q[j + 1])
                    + factors[1, j + 1] * jnp.where(forward, u[j], v[j + 1])
                    + factors[2, j + 1] * jnp.where(forward, v[j], u[j + 1])
                )
            if 0 <= j < count:
                swept[rows(8 * i + j + shift)] = q[j] - (sent[j] - sent[j - 1]) * per_mass[rows(j + 3)]

    open_y = lax.broadcasted_iota(jnp.int32, (8, 128), 1) < 127
    substeps = level(tables, window, 0)
    for k in range(8):
        r = level(per_mass, 3 - shift, k)
        fy = jnp.where(open_y, flux_y(k), 0.0)
        y1, y2 = face_factors(fy, r, pltpu.roll(r, 127, 1))
        lines[0, k], lines[1, k], lines[2, k], lines[3, k] = r, fy, y1, y2
        if k > 0:
            fz = flux_z(k - 1)
            z1, z2 = face_factors(fz, r_below, r)
            lines[4, k - 1], lines[5, k - 1], lines[6, k - 1] = fz, z1, z2
            rate = level(tables, window, k)
            lines[7, k] = rate
            lines[8, k] = jnp.where(substeps > 1.5, rate, 0.0)
            lines[9, k] = jnp.where(substeps > 2.5, rate, 0.0)
        r_below = r

    for i in range(4):
        q = [level(swept, 8 * i, k) for k in range(8)]
        q = [sweep_y(q[k], lines[1, k], lines[2, k], lines[3, k], lines[0, k], open_y) for k in range(8)]
        q = sweep_z(q, lambda k: (lines[4, k], lines[5, k], lines[6, k]), lambda k: lines[0, k])
        for m in (7, 8, 9):
            up = [None] + [lines[m, k] for k in range(1, 8)]
            q = [
                (q[k] * (1.0 - up[k + 1]) if k < 7 else q[k]) + (up[k] * q[k - 1] if k > 0 else 0.0)
                for k in range(8)
            ]
        for k in range(8):
            emit(i, k, q[k])


def near_kernel(
    met_ref, tracers_ref, conv_ref, mate_ref, out_ref,
    cells, fx_0, mass_0, fy_0, fz_0, tables, swept, factors, per_mass, lines,
):
    core = lax.axis_index("core")
    wide = {(FX, 0): fx_0, (MASS, 0): mass_0, (FY, 0): fy_0, (FZ, 0): fz_0}
    stage(wide, cells, tables, met_ref, tracers_ref, conv_ref, ((lambda n: mate_ref[1 - core, n], lambda n: mate_ref[1 - core, BODY + n], 1 - core),))
    base = 6 * (1 - core)

    def emit(i, k, q):
        out_ref[pl.ds(64 * i + k, 8, stride=8), :] = q

    advance(
        8, 0, lambda i, n: cells[rows(20 * i + base + n)], lambda n: fx_0[rows(base + n)], lambda n: mass_0[rows(base + n)],
        lambda k: level(fy_0, base, k), lambda k: level(fz_0, base, k), tables, base, emit, swept, factors, per_mass, lines,
    )


def far_kernel(
    met_ref, tracers_ref, conv_ref, mate_ref, bulk_ref, far_ref, near_ref, out_ref,
    cells, fx_0, mass_0, fy_0, fz_0, fx_1, mass_1, tables, state, swept, factors, per_mass, lines,
):
    core = lax.axis_index("core")
    wide = {(FX, 0): fx_0, (MASS, 0): mass_0, (FY, 0): fy_0, (FZ, 0): fz_0}
    far = (lambda n: bulk_ref[n], lambda n: far_ref[n], core)
    mate = (None, lambda n: mate_ref[1 - core, BODY + n], 1 - core)
    stage(wide, cells, tables, met_ref, tracers_ref, conv_ref, (far,))
    stage({(FX, 1): fx_1, (MASS, 1): mass_1}, None, None, met_ref, None, None, (far, mate))
    base, window = 8 * core, 6 * core

    def keep(i, k, q):
        state[pl.ds(8 * (14 * i + window) + k, 8, stride=8), :] = q

    advance(
        6, 2 * core, lambda i, n: cells[rows(20 * i + base + n)], lambda n: fx_0[rows(base + n)], lambda n: mass_0[rows(base + n)],
        lambda k: level(fy_0, window, k), lambda k: level(fz_0, window, k), tables, window, keep, swept, factors, per_mass, lines,
    )
    for i in range(4):
        for n in range(8):
            state[rows(14 * i + 6 * (1 - core) + n)] = near_ref[rows(8 * i + n)]

    def emit(i, k, q):
        out_ref[rows(8 * i + k)] = q

    advance(
        8, 0, lambda i, n: state[rows(14 * i + n)], lambda n: fx_1[rows(n)], lambda n: mass_1[rows(n)],
        lambda k: level(met_ref, 32 + 8 * FY, k), lambda k: level(met_ref, 32 + 8 * FZ, k), tables, 3, emit, swept, factors, per_mass, lines,
    )


def body(tracers, flux_pool, mass_pool, owner, conv_cols, conv_steps, conv_rate):
    packed, owners, dense = call(
        pack_kernel, (shaped(64, 8, 128), shaped(2, 8, 128, dtype=jnp.int32), shaped(8, 8, 128)),
        flux_pool.reshape(384, 128), mass_pool.reshape(128, 128), owner.reshape(1, 2),
        conv_cols, conv_steps, conv_rate.reshape(7, 1, 256), near=False,
    )
    lines = tracers.reshape(256, 128)
    size = lax.axis_size(TILE)
    distant = [(i, (i + 2 * (i % 2) - 1) % size) for i in range(size)]
    body_far, body_mate = call(send_body_kernel, (shaped(BODY, 8, 128), shaped(BODY, 8, 128)), lines, dense)
    dealt = lax.all_to_all(packed, NEAR, 0, 0, tiled=True)
    far_bulk = lax.ppermute(body_far, TILE, distant)
    third = call(functools.partial(pick_kernel, which=0), shaped(24, 8, 128), owners, dealt)
    thirds = lax.all_to_all(third, "za", 0, 0, tiled=True)
    own = call(functools.partial(pick_kernel, which=1), shaped(64, 8, 128), owners, thirds)
    met = lax.all_to_all(own, NEAR, 0, 0, tiled=True)
    to_far, to_mate = call(send_met_kernel, (shaped(SENT - BODY, 8, 128), shaped(SENT, 8, 128)), met, body_mate)
    from_far = lax.ppermute(to_far, TILE, distant)
    from_mate = lax.all_gather(to_mate, "core")

    def columns(n):
        return pltpu.VMEM((8 * n, 128), F32)

    met = met.reshape(512, 128)
    arrays = [columns(80)] + [columns(8 + 2 * k) for _, _, k in HALO[:4]]
    work = [columns(32), pltpu.VMEM((3, 9, 8, 128), F32), columns(12), pltpu.VMEM((10, 8, 8, 128), F32)]
    ahead = call(
        near_kernel, shaped(256, 128), met, lines, dense, from_mate,
        scratch=arrays + [columns(14)] + work, flops=3000000,
    )
    out = call(
        far_kernel, jax.ShapeDtypeStruct((256, 128), F32), met, lines, dense, from_mate, far_bulk, from_far, ahead,
        scratch=arrays + [columns(10)] * 2 + [columns(14), columns(56)] + work, flops=5000000,
    )
    return out.reshape(tracers.shape)


def solution(mesh):
    split = Mesh(mesh.devices.reshape(2, 8, 2, 2, 3, 4), TILE + TRC)
    in_specs = (
        P(TRC, None, TILE, None),
        P(TRC, None, None, None, TILE, None),
        P(TRC, None, None, TILE, None),
        P(None, TILE),
        P(TILE, None),
        P(TILE, None),
        P(TILE, None, None),
    )
    out_specs = P(TRC, None, TILE, None)
    return jax.shard_map(body, mesh=split, in_specs=in_specs, out_specs=out_specs, check_vma=False)
```

profile of v0, /device:TPU:4, one launch (start us, length us, event | category | flops | bytes accessed | tf_op | source)
XLA Modules:
  0.0 62.8 jit_solution(6226585953715108147)
XLA Ops:
  0.0 1.3 %shard_map.73 = (f32[64,8,128]{2,1,0:T(8,128)S(1)}, s32[2,8,128]{2,1,0:T(8,128)S(1)}, f32[8,8,128]{2,1,0:T(8,128)S(1)}) custom-call(f32[384,128]{1,0:T(8,128)} %bitcast.15, f32[128,128]{1,0:T(8,128)} %bitcast.16, s32[1,2]{1,0:T(1,128)} %bitcast.18, s32[1,256]{1,0:T(1,128)} %cols_ref.1, s32[1,256]{1,0:T(1,128)} %steps_ref.1, f32[7,1,256]{2,1,0:T(1,128)} %bitcast.17), custom_call_target="tpu_custom_call" | custom-call | flops 20000 | bytes 271368 | tf_op jit(solution)/shard_map/pallas_call | solution.py:23
  1.3 17.5 %all_to_all.15.got_ref = f32[64,8,128]{2,1,0:T(8,128)S(1)} all-to-all(f32[64,8,128]{2,1,0:T(8,128)S(1)} %get-tuple-element.13), channel_id=1, replica_groups=mesh['x_hi'=2,'y'=8,'core'=2,'x_lo'=2,'za'=3,'zb'=4] {'x_lo','zb'}, dimensions={0} | all-to-all | bytes 524288 | tf_op jit(solution)/shard_map/all_to_all | solution.py:329
  18.8 19.7 %all_to_all.16.got_ref = f32[24,8,128]{2,1,0:T(8,128)S(1)} all-to-all(f32[24,8,128]{2,1,0:T(8,128)S(1)} %shard_map.74), channel_id=1, replica_groups=mesh['x_hi'=2,'y'=8,'core'=2,'x_lo'=2,'za'=3,'zb'=4] {'za'}, dimensions={0} | all-to-all | bytes 196608 | tf_op jit(solution)/shard_map/all_to_all | solution.py:332
  38.5 0.7 %shard_map.75 = f32[64,8,128]{2,1,0:T(8,128)} custom-call(s32[2,8,128]{2,1,0:T(8,128)S(1)} %get-tuple-element.12.owner_ref, f32[24,8,128]{2,1,0:T(8,128)S(1)} %all_to_all.16.got_ref), custom_call_target="tpu_custom_call" | custom-call | flops 20000 | bytes 106496 | tf_op jit(solution)/shard_map/pallas_call | solution.py:23
  39.3 0.0 copy-start
  39.3 3.5 %all-to-all-start.2 = ((f32[64,8,128]{2,1,0:T(8,128)}), f32[64,8,128]{2,1,0:T(8,128)S(1)}, u32[]{:S(2)}, u32[]{:S(2)}) async-start(f32[64,8,128]{2,1,0:T(8,128)} %shard_map.75), calls=%async_computation.2 | async-start | bytes 524288 | tf_op jit(solution)/shard_map/all_to_all | solution.py:334
  42.8 0.0 copy-done
  42.8 0.1 shard_map.76
  42.9 2.6 %collective-permute-start = (f32[27,8,128]{2,1,0:T(8,128)S(1)}, f32[27,8,128]{2,1,0:T(8,128)S(1)}, u32[]{:S(2)}, u32[]{:S(2)}) collective-permute-start(f32[27,8,128]{2,1,0:T(8,128)S(1)} %get-tuple-element.17), channel_id=1, source_target_pairs={{0,744},{24,48},{48,24},{72,96},{96,72},{120,144},{144,120},{168,1... | collective-permute-start | bytes 331784 | tf_op jit(solution)/shard_map/ppermute | solution.py:330
  45.5 6.0 %all-to-all-done.2.met_ref = f32[64,8,128]{2,1,0:T(8,128)S(1)} async-done(((f32[64,8,128]{2,1,0:T(8,128)}), f32[64,8,128]{2,1,0:T(8,128)S(1)}, u32[]{:S(2)}, u32[]{:S(2)}) %all-to-all-start.2) | async-done | bytes 262176 | tf_op jit(solution)/shard_map/all_to_all | solution.py:334
  51.5 1.9 %collective-permute-start.1 = (f32[16,8,128]{2,1,0:T(8,128)S(1)}, f32[16,8,128]{2,1,0:T(8,128)S(1)}, u32[]{:S(2)}, u32[]{:S(2)}) collective-permute-start(f32[16,8,128]{2,1,0:T(8,128)S(1)} %get-tuple-element.18), channel_id=1, source_target_pairs={{0,744},{24,48},{48,24},{72,96},{96,72},{120,144},{144,120},{168,1... | collective-permute-start | bytes 196616 | tf_op jit(solution)/shard_map/ppermute | solution.py:336
  53.4 3.2 %all-gather = f32[86,8,128]{2,1,0:T(8,128)S(1)} all-gather(f32[43,8,128]{2,1,0:T(8,128)S(1)} %get-tuple-element.16), channel_id=2, replica_groups=mesh['x_hi'=2,'y'=8,'core'=2,'x_lo'=2,'za'=3,'zb'=4] {'core'}, dimensions={0}, use_global_device_ids=true | all-gather | bytes 528384 | tf_op jit(solution)/shard_map/all_gather | solution.py:337
  56.6 0.8 %shard_map.78.near_ref = f32[256,128]{1,0:T(8,128)S(1)} custom-call(f32[512,128]{1,0:T(8,128)S(1)} %bitcast.8, f32[256,128]{1,0:T(8,128)S(1)} %bitcast.13, f32[8,8,128]{2,1,0:T(8,128)S(1)} %get-tuple-element.14.conv_ref, f32[2,43,8,128]{3,2,1,0:T(8,128)S(1)} %bitcast.10), custom_call_target="tpu_custom_call" | custom-call | flops 3000000 | bytes 778240 | tf_op jit(solution)/shard_map/pallas_call | solution.py:23
  57.4 0.0 collective-permute-done.bulk_ref
  57.4 3.3 %collective-permute-done.1.far_ref = f32[16,8,128]{2,1,0:T(8,128)S(1)} collective-permute-done((f32[16,8,128]{2,1,0:T(8,128)S(1)}, f32[16,8,128]{2,1,0:T(8,128)S(1)}, u32[]{:S(2)}, u32[]{:S(2)}) %collective-permute-start.1) | collective-permute-done | bytes 65568 | tf_op jit(solution)/shard_map/ppermute | solution.py:336
  60.7 2.1 %shard_map.79 = f32[256,128]{1,0:T(8,128)} custom-call(f32[512,128]{1,0:T(8,128)S(1)} %bitcast.9, f32[256,128]{1,0:T(8,128)S(1)} %bitcast.14, f32[8,8,128]{2,1,0:T(8,128)S(1)} %get-tuple-element.14.conv_ref, f32[2,43,8,128]{3,2,1,0:T(8,128)S(1)} %bitcast.11, f32[27,8,128]{2,1,0:T(8,128)S(1)} %collective-permute-done.bulk_ref, ...), custom_call_target="tpu_custom_call" | custom-call | flops 5000000 | bytes 1085440 | tf_op jit(solution)/shard_map/pallas_call | solution.py:23
  (2 shorter events, 0.0 us)
Async XLA Ops:
  39.3 3.6 %copy-start = (f32[4,8,8,128]{3,2,1,0:T(8,128)S(1)}, f32[4,8,8,128]{3,2,1,0:T(8,128)}, u32[]{:S(2)}) copy-start(f32[4,8,8,128]{3,2,1,0:T(8,128)} %param.7) | copy-start | bytes 393220
  39.3 12.2 %all-to-all-start.2 = ((f32[64,8,128]{2,1,0:T(8,128)}), f32[64,8,128]{2,1,0:T(8,128)S(1)}, u32[]{:S(2)}, u32[]{:S(2)}) async-start(f32[64,8,128]{2,1,0:T(8,128)} %shard_map.75), calls=%async_computation.2 | async-start | bytes 524288 | tf_op jit(solution)/shard_map/all_to_all | solution.py:334
  42.9 14.6 %collective-permute-start = (f32[27,8,128]{2,1,0:T(8,128)S(1)}, f32[27,8,128]{2,1,0:T(8,128)S(1)}, u32[]{:S(2)}, u32[]{:S(2)}) collective-permute-start(f32[27,8,128]{2,1,0:T(8,128)S(1)} %get-tuple-element.17), channel_id=1, source_target_pairs={{0,744},{24,48},{48,24},{72,96},{96,72},{120,144},{144,120},{168,1... | collective-permute-start | bytes 331784 | tf_op jit(solution)/shard_map/ppermute | solution.py:330
  51.5 9.2 %collective-permute-start.1 = (f32[16,8,128]{2,1,0:T(8,128)S(1)}, f32[16,8,128]{2,1,0:T(8,128)S(1)}, u32[]{:S(2)}, u32[]{:S(2)}) collective-permute-start(f32[16,8,128]{2,1,0:T(8,128)S(1)} %get-tuple-element.18), channel_id=1, source_target_pairs={{0,744},{24,48},{48,24},{72,96},{96,72},{120,144},{144,120},{168,1... | collective-permute-start | bytes 196616 | tf_op jit(solution)/shard_map/ppermute | solution.py:336
where the time goes:
time: 63.1 us; the launch traced here: 62.8 us
  blocking collectives  40.4 us (64%)
  waiting for transfers between devices  9.21 us (15%)
  starting transfers between devices  8.09 us (13%)
  Pallas kernels  4.95 us (8%)
    all_to_all x1, blocking collectives, body(): thirds = lax.all_to_all(third, 'za', 0, 0, tiled=True)  19.7 us
    all_to_all x1, blocking collectives, body(): dealt = lax.all_to_all(packed, NEAR, 0, 0, tiled=True)  17.5 us
    all_to_all x1, waiting for transfers between devices, body(): met = lax.all_to_all(own, NEAR, 0, 0, tiled=True)  5.95 us
    pallas_call x7, Pallas kernels, call(): pl.pallas_call(kernel, out_shape=outs, in_specs=[VM] * len(args), out_spe...  4.95 us
    all_to_all x1, starting transfers between devices, body(): met = lax.all_to_all(own, NEAR, 0, 0, tiled=True)  3.54 us
    ppermute x1, waiting for transfers between devices, body(): from_far = lax.ppermute(to_far, TILE, distant)  3.25 us
    all_gather x1, blocking collectives, body(): from_mate = lax.all_gather(to_mate, 'core')  3.22 us
    ppermute x1, starting transfers between devices, body(): far_bulk = lax.ppermute(body_far, TILE, distant)  2.63 us
  transfers between devices with their start and end apart: 3, of which 2 were waited for; matrix products, arithmetic and copies ran while one was open for 0% of the time, Pallas kernels for 1%

commit v1 on v0

--- a/solution.py
+++ b/solution.py
@@ -34,7 +34,7 @@
     return ref[pl.ds(first + x, 8, stride=8), :]
 
 
-def pack_kernel(flux_ref, mass_ref, owner_ref, cols_ref, steps_ref, rate_ref, out_ref, owner_out, dense_ref):
+def pack_kernel(flux_ref, mass_ref, owner_ref, out_ref, owner_out):
     for s in range(2):
         for x in range(8):
             for f in range(3):
@@ -44,16 +44,6 @@
     owner = jnp.broadcast_to(jnp.where(first, owner_ref[0:1, 0:1], owner_ref[0:1, 1:2]), (8, 128))
     owner_out[0] = 4 * (owner // 12) + owner % 4
     owner_out[1] = (owner % 12) // 4
-    cols = cols_ref[...]
-    at_x, at_y = cols // 128, cols % 128
-    values = jnp.concatenate([steps_ref[...].astype(F32), rate_ref[:, 0, :]], axis=0)
-    weights = jnp.concatenate([jnp.where(at_x == x, values, 0.0) for x in range(8)], axis=0)
-    hot = jnp.where(lax.broadcasted_iota(jnp.int32, (128, cols.shape[1]), 0) == at_y, 1.0, 0.0)
-    dense = lax.dot_general(
-        weights, hot, (((1,), (1,)), ((), ())),
-        precision=lax.Precision.HIGHEST, preferred_element_type=F32,
-    )
-    dense_ref[...] = dense.reshape(dense_ref.shape)
 
 
 def pick_kernel(owner_ref, got_ref, out_ref, *, which):
@@ -92,10 +82,20 @@
         at += k
 
 
-def send_body_kernel(tracers_ref, conv_ref, far_ref, mate_ref):
+def send_body_kernel(tracers_ref, cols_ref, steps_ref, rate_ref, far_ref, mate_ref, dense_ref):
+    cols = cols_ref[...]
+    at_x, at_y = cols // 128, cols % 128
+    values = jnp.concatenate([steps_ref[...].astype(F32), rate_ref[:, 0, :]], axis=0)
+    weights = jnp.concatenate([jnp.where(at_x == x, values, 0.0) for x in range(8)], axis=0)
+    hot = jnp.where(lax.broadcasted_iota(jnp.int32, (128, cols.shape[1]), 0) == at_y, 1.0, 0.0)
+    dense = lax.dot_general(
+        weights, hot, (((1,), (1,)), ((), ())),
+        precision=lax.Precision.HIGHEST, preferred_element_type=F32,
+    )
+    dense_ref[...] = dense.reshape(dense_ref.shape)
     core = lax.axis_index("core")
-    fill_body(far_ref, core, tracers_ref, conv_ref)
-    fill_body(mate_ref, 1 - core, tracers_ref, conv_ref)
+    fill_body(far_ref, core, tracers_ref, dense_ref)
+    fill_body(mate_ref, 1 - core, tracers_ref, dense_ref)
 
 
 def send_met_kernel(met_ref, body_ref, far_ref, mate_ref):
@@ -317,15 +317,17 @@
 
 
 def body(tracers, flux_pool, mass_pool, owner, conv_cols, conv_steps, conv_rate):
-    packed, owners, dense = call(
-        pack_kernel, (shaped(64, 8, 128), shaped(2, 8, 128, dtype=jnp.int32), shaped(8, 8, 128)),
-        flux_pool.reshape(384, 128), mass_pool.reshape(128, 128), owner.reshape(1, 2),
-        conv_cols, conv_steps, conv_rate.reshape(7, 1, 256), near=False,
+    packed, owners = call(
+        pack_kernel, (shaped(64, 8, 128), shaped(2, 8, 128, dtype=jnp.int32)),
+        flux_pool.reshape(384, 128), mass_pool.reshape(128, 128), owner.reshape(1, 2), near=False,
     )
     lines = tracers.reshape(256, 128)
     size = lax.axis_size(TILE)
     distant = [(i, (i + 2 * (i % 2) - 1) % size) for i in range(size)]
-    body_far, body_mate = call(send_body_kernel, (shaped(BODY, 8, 128), shaped(BODY, 8, 128)), lines, dense)
+    body_far, body_mate, dense = call(
+        send_body_kernel, (shaped(BODY, 8, 128), shaped(BODY, 8, 128), shaped(8, 8, 128)),
+        lines, conv_cols, conv_steps, conv_rate.reshape(7, 1, 256),
+    )
     dealt = lax.all_to_all(packed, NEAR, 0, 0, tiled=True)
     far_bulk = lax.ppermute(body_far, TILE, distant)
     third = call(functools.partial(pick_kernel, which=0), shaped(24, 8, 128), owners, dealt)

time: 63.1 us -> 62.9 us (level)
  waiting for transfers between devices: 9.21 us -> 8.04 us
  local copies, waits for them, and re-layouts: 0.01 us -> 0.66 us
    all_to_all x1, waiting for transfers between devices: 5.95 us -> 4.93 us  [body(): met = lax.all_to_all(own, NEAR, 0, 0, tiled=True)]
    unnamed x2 -> x8, local copies, waits for them, and re-layouts: 0.01 us -> 0.66 us
  transfers between devices with their start and end apart: 3 -> 3, of which waited for: 2 -> 2; matrix products, arithmetic and copies ran while one was open for 0% -> 0% of each run, Pallas kernels for 1% -> 2%
where the time goes in v1:
time: 62.9 us; the launch traced here: 62.5 us
  blocking collectives  40.6 us (65%)
  starting transfers between devices  8.09 us (13%)
  waiting for transfers between devices  8.04 us (13%)
  Pallas kernels  5.02 us (8%)
  local copies, waits for them, and re-layouts  0.66 us (1%)
    all_to_all x1, blocking collectives, body(): thirds = lax.all_to_all(third, 'za', 0, 0, tiled=True)  19.7 us
    all_to_all x1, blocking collectives, body(): dealt = lax.all_to_all(packed, NEAR, 0, 0, tiled=True)  17.5 us
    pallas_call x7, Pallas kernels, call(): pl.pallas_call(kernel, out_shape=outs, in_specs=[VM] * len(args), out_spe...  5.02 us
    all_to_all x1, waiting for transfers between devices, body(): met = lax.all_to_all(own, NEAR, 0, 0, tiled=True)  4.93 us
    all_to_all x1, starting transfers between devices, body(): met = lax.all_to_all(own, NEAR, 0, 0, tiled=True)  3.54 us
    all_gather x1, blocking collectives, body(): from_mate = lax.all_gather(to_mate, 'core')  3.37 us
    ppermute x1, waiting for transfers between devices, body(): from_far = lax.ppermute(to_far, TILE, distant)  3.1 us
    ppermute x1, starting transfers between devices, body(): far_bulk = lax.ppermute(body_far, TILE, distant)  2.63 us
  transfers between devices with their start and end apart: 3, of which 2 were waited for; matrix products, arithmetic and copies ran while one was open for 0% of the time, Pallas kernels for 2%

profile of v1, /device:TPU:4, one launch (start us, length us, event | category | flops | bytes accessed | tf_op | source)
XLA Modules:
  0.0 62.5 jit_solution(5674696967329477108)
XLA Ops:
  0.0 1.2 %shard_map.73 = (f32[64,8,128]{2,1,0:T(8,128)S(1)}, s32[2,8,128]{2,1,0:T(8,128)S(1)}) custom-call(f32[384,128]{1,0:T(8,128)} %bitcast.16, f32[128,128]{1,0:T(8,128)} %bitcast.17, s32[1,2]{1,0:T(1,128)} %bitcast.18), custom_call_target="tpu_custom_call" | custom-call | flops 20000 | bytes 262152 | tf_op jit(solution)/shard_map/pallas_call | solution.py:23
  1.2 17.5 %all_to_all.15.got_ref = f32[64,8,128]{2,1,0:T(8,128)S(1)} all-to-all(f32[64,8,128]{2,1,0:T(8,128)S(1)} %get-tuple-element.13), channel_id=1, replica_groups=mesh['x_hi'=2,'y'=8,'core'=2,'x_lo'=2,'za'=3,'zb'=4] {'x_lo','zb'}, dimensions={0} | all-to-all | bytes 524288 | tf_op jit(solution)/shard_map/all_to_all | solution.py:331
  18.7 19.7 %all_to_all.16.got_ref = f32[24,8,128]{2,1,0:T(8,128)S(1)} all-to-all(f32[24,8,128]{2,1,0:T(8,128)S(1)} %shard_map.74), channel_id=1, replica_groups=mesh['x_hi'=2,'y'=8,'core'=2,'x_lo'=2,'za'=3,'zb'=4] {'za'}, dimensions={0} | all-to-all | bytes 196608 | tf_op jit(solution)/shard_map/all_to_all | solution.py:334
  38.4 0.7 %shard_map.75 = f32[64,8,128]{2,1,0:T(8,128)} custom-call(s32[2,8,128]{2,1,0:T(8,128)S(1)} %get-tuple-element.12.owner_ref, f32[24,8,128]{2,1,0:T(8,128)S(1)} %all_to_all.16.got_ref), custom_call_target="tpu_custom_call" | custom-call | flops 20000 | bytes 106496 | tf_op jit(solution)/shard_map/pallas_call | solution.py:23
  39.1 0.0 copy-start
  39.1 0.0 copy-start.1
  39.1 0.0 copy-start.3
  39.1 3.5 %all-to-all-start.2 = ((f32[64,8,128]{2,1,0:T(8,128)}), f32[64,8,128]{2,1,0:T(8,128)S(1)}, u32[]{:S(2)}, u32[]{:S(2)}) async-start(f32[64,8,128]{2,1,0:T(8,128)} %shard_map.75), calls=%async_computation.2 | async-start | bytes 524288 | tf_op jit(solution)/shard_map/all_to_all | solution.py:336
  42.7 0.0 copy-start.2
  42.7 0.0 copy-done
  42.7 0.0 copy-done.1
  42.7 0.0 copy-done.3
  42.7 0.6 %copy-done.2 = s32[1,256]{1,0:T(1,128)S(1)} copy-done((s32[1,256]{1,0:T(1,128)S(1)}, s32[1,256]{1,0:T(1,128)}, u32[]{:S(2)}) %copy-start.2) | copy-done | bytes 1048
  43.4 0.3 shard_map.76
  43.6 2.6 %collective-permute-start = (f32[27,8,128]{2,1,0:T(8,128)S(1)}, f32[27,8,128]{2,1,0:T(8,128)S(1)}, u32[]{:S(2)}, u32[]{:S(2)}) collective-permute-start(f32[27,8,128]{2,1,0:T(8,128)S(1)} %get-tuple-element.17), channel_id=1, source_target_pairs={{0,744},{24,48},{48,24},{72,96},{96,72},{120,144},{144,120},{168,1... | collective-permute-start | bytes 331784 | tf_op jit(solution)/shard_map/ppermute | solution.py:332
  46.3 4.9 %all-to-all-done.2.met_ref = f32[64,8,128]{2,1,0:T(8,128)S(1)} async-done(((f32[64,8,128]{2,1,0:T(8,128)}), f32[64,8,128]{2,1,0:T(8,128)S(1)}, u32[]{:S(2)}, u32[]{:S(2)}) %all-to-all-start.2) | async-done | bytes 262176 | tf_op jit(solution)/shard_map/all_to_all | solution.py:336
  51.2 1.9 %collective-permute-start.1 = (f32[16,8,128]{2,1,0:T(8,128)S(1)}, f32[16,8,128]{2,1,0:T(8,128)S(1)}, u32[]{:S(2)}, u32[]{:S(2)}) collective-permute-start(f32[16,8,128]{2,1,0:T(8,128)S(1)} %get-tuple-element.18), channel_id=1, source_target_pairs={{0,744},{24,48},{48,24},{72,96},{96,72},{120,144},{144,120},{168,1... | collective-permute-start | bytes 196616 | tf_op jit(solution)/shard_map/ppermute | solution.py:338
  53.2 3.4 %all-gather = f32[86,8,128]{2,1,0:T(8,128)S(1)} all-gather(f32[43,8,128]{2,1,0:T(8,128)S(1)} %get-tuple-element.16), channel_id=2, replica_groups=mesh['x_hi'=2,'y'=8,'core'=2,'x_lo'=2,'za'=3,'zb'=4] {'core'}, dimensions={0}, use_global_device_ids=true | all-gather | bytes 528384 | tf_op jit(solution)/shard_map/all_gather | solution.py:339
  56.5 0.8 %shard_map.78.near_ref = f32[256,128]{1,0:T(8,128)S(1)} custom-call(f32[512,128]{1,0:T(8,128)S(1)} %bitcast.8, f32[256,128]{1,0:T(8,128)S(1)} %bitcast.13, f32[8,8,128]{2,1,0:T(8,128)S(1)} %get-tuple-element.14.conv_ref, f32[2,43,8,128]{3,2,1,0:T(8,128)S(1)} %bitcast.10), custom_call_target="tpu_custom_call" | custom-call | flops 3000000 | bytes 778240 | tf_op jit(solution)/shard_map/pallas_call | solution.py:23
  57.3 0.0 collective-permute-done.bulk_ref
  57.3 3.1 %collective-permute-done.1.far_ref = f32[16,8,128]{2,1,0:T(8,128)S(1)} collective-permute-done((f32[16,8,128]{2,1,0:T(8,128)S(1)}, f32[16,8,128]{2,1,0:T(8,128)S(1)}, u32[]{:S(2)}, u32[]{:S(2)}) %collective-permute-start.1) | collective-permute-done | bytes 65568 | tf_op jit(solution)/shard_map/ppermute | solution.py:338
  60.4 2.1 %shard_map.79 = f32[256,128]{1,0:T(8,128)} custom-call(f32[512,128]{1,0:T(8,128)S(1)} %bitcast.9, f32[256,128]{1,0:T(8,128)S(1)} %bitcast.14, f32[8,8,128]{2,1,0:T(8,128)S(1)} %get-tuple-element.14.conv_ref, f32[2,43,8,128]{3,2,1,0:T(8,128)S(1)} %bitcast.11, f32[27,8,128]{2,1,0:T(8,128)S(1)} %collective-permute-done.bulk_ref, ...), custom_call_target="tpu_custom_call" | custom-call | flops 5000000 | bytes 1085440 | tf_op jit(solution)/shard_map/pallas_call | solution.py:23
  (2 shorter events, 0.0 us)
Async XLA Ops:
  39.1 3.6 %copy-start = (f32[4,8,8,128]{3,2,1,0:T(8,128)S(1)}, f32[4,8,8,128]{3,2,1,0:T(8,128)}, u32[]{:S(2)}) copy-start(f32[4,8,8,128]{3,2,1,0:T(8,128)} %param.7) | copy-start | bytes 393220
  39.1 3.6 %copy-start.1 = (f32[1,7,256]{2,0,1:T(1,128)S(1)}, f32[1,7,256]{2,0,1:T(1,128)}, u32[]{:S(2)}) copy-start(f32[1,7,256]{2,0,1:T(1,128)} %param.13) | copy-start | bytes 21508
  39.1 3.6 %copy-start.3 = (s32[1,256]{1,0:T(1,128)S(1)}, s32[1,256]{1,0:T(1,128)}, u32[]{:S(2)}) copy-start(s32[1,256]{1,0:T(1,128)} %steps_ref.1) | copy-start | bytes 3076
  39.1 12.1 %all-to-all-start.2 = ((f32[64,8,128]{2,1,0:T(8,128)}), f32[64,8,128]{2,1,0:T(8,128)S(1)}, u32[]{:S(2)}, u32[]{:S(2)}) async-start(f32[64,8,128]{2,1,0:T(8,128)} %shard_map.75), calls=%async_computation.2 | async-start | bytes 524288 | tf_op jit(solution)/shard_map/all_to_all | solution.py:336
  42.7 0.7 %copy-start.2 = (s32[1,256]{1,0:T(1,128)S(1)}, s32[1,256]{1,0:T(1,128)}, u32[]{:S(2)}) copy-start(s32[1,256]{1,0:T(1,128)} %cols_ref.1) | copy-start | bytes 3076
  43.6 13.7 %collective-permute-start = (f32[27,8,128]{2,1,0:T(8,128)S(1)}, f32[27,8,128]{2,1,0:T(8,128)S(1)}, u32[]{:S(2)}, u32[]{:S(2)}) collective-permute-start(f32[27,8,128]{2,1,0:T(8,128)S(1)} %get-tuple-element.17), channel_id=1, source_target_pairs={{0,744},{24,48},{48,24},{72,96},{96,72},{120,144},{144,120},{168,1... | collective-permute-start | bytes 331784 | tf_op jit(solution)/shard_map/ppermute | solution.py:332
  51.2 9.2 %collective-permute-start.1 = (f32[16,8,128]{2,1,0:T(8,128)S(1)}, f32[16,8,128]{2,1,0:T(8,128)S(1)}, u32[]{:S(2)}, u32[]{:S(2)}) collective-permute-start(f32[16,8,128]{2,1,0:T(8,128)S(1)} %get-tuple-element.18), channel_id=1, source_target_pairs={{0,744},{24,48},{48,24},{72,96},{96,72},{120,144},{144,120},{168,1... | collective-permute-start | bytes 196616 | tf_op jit(solution)/shard_map/ppermute | solution.py:338
